TPU v7x, 32 devices: a whole 2x2x4 slice. The times are simulated.
32 devices in a mesh: dp: 8 (over z, y), rep: 4 (over x, core).
Axes of the slice: x: 2, y: 2, z: 4, core: 2. Of those that a mesh axis runs over, the one named last changes fastest.
Arguments:
- packet_bytes: int32 [4096, 256], P(('dp', 'rep')), may hold values from 0 to 255
- owner_index: int32 [4096], P(('dp', 'rep')), may hold values from 0 to 7, as said below
- session_id: int32 [4096], P(('dp', 'rep')), may hold values from 0 to 15
- class_label: int32 [512], P(('dp', 'rep')), may hold values from 0 to 127
- byte_table: bfloat16 [256, 64], replicated, may hold values from -6 to 6
- w_conv: bfloat16 [512, 512], replicated, may hold values from -0.25 to 0.25
- norm_gain: bfloat16 [512], replicated, may hold values from 0.099609375 to 1.8984375
- w_project: bfloat16 [512, 1536], replicated, may hold values from -7 to 7
- w_out: bfloat16 [512, 512], replicated, may hold values from -0.25 to 0.25
- w_head: bfloat16 [512, 128], replicated, may hold values from -4 to 4
Outputs:
- logits: float32 [512, 128], P(('dp', 'rep'))
- grad_table: float32 [256, 64], replicated
- grad_conv: float32 [512, 512], replicated
- grad_gain: float32 [512], replicated
- grad_project: float32 [512, 1536], replicated
- grad_out: float32 [512, 512], replicated
- grad_head: float32 [512, 128], replicated
Inputs may be any that keep to these rules, and one draw needn't show every extreme that they name: `owner_index`: of one device's packets at most 32 name any one owner; in each group along dp one owner is named by exactly 32 packets of every device of the group.
All inputs are finite; a program needn't handle non-finite values.
Results may differ from a plain program's by a relative error of at most 0.01.
Values may be sent and summed in bfloat16 or wider, within the bound.
No kernel may reach another device: no remote copies, remote signals or barrier semaphores. Data moves between devices by JAX's collectives and lax.ppermute only.
A program may use at most 128 MiB of HBM per device.

v0:
```python
import jax
import jax.numpy as jnp
from jax import lax
from jax.sharding import PartitionSpec as P

BYTES = 256
KERNEL = 8
HEADS = 8
SESS = 16
NORM_EPS = 1e-06


def silu_slope(values_in):
    sigma = jax.nn.sigmoid(values_in)
    return sigma * (1.0 + values_in * (1.0 - sigma))


def lookup_block(block_codes, byte_table):
    vocab = lax.broadcasted_iota(jnp.int32, (1, 1, 256), 2)
    onehot = (block_codes[:, :, None] == vocab).astype(jnp.bfloat16)
    return jnp.einsum("pbv,vc->pbc", onehot, byte_table, preferred_element_type=jnp.float32).astype(
        jnp.bfloat16
    )


def windows_of(byte_codes, byte_table):
    packets, length = byte_codes.shape
    blocks = byte_codes.reshape(packets // 16, 16, length)
    feats = lax.map(lambda block_codes: lookup_block(block_codes, byte_table), blocks)
    return feats.reshape(packets, length // KERNEL, KERNEL * byte_table.shape[1])


def session_layer(received, recv_session, labels_here, norm_gain, w_project, w_out, w_head):
    f32 = jnp.float32
    bf16 = jnp.bfloat16
    slot_count, model_width = received.shape
    head_dim = model_width // HEADS
    score_scale = head_dim ** (-0.5)
    as_float = received.astype(f32)
    inverse = lax.rsqrt(jnp.mean(as_float * as_float, axis=1, keepdims=True) + NORM_EPS)
    gain_f = norm_gain.astype(f32)
    norm_in = (as_float * inverse * gain_f).astype(bf16)
    projected = jnp.dot(norm_in, w_project, preferred_element_type=f32).astype(bf16)
    projected = projected.reshape(slot_count, 3, HEADS, head_dim)
    queries = projected[:, 0]
    keys_all = projected[:, 1]
    values = projected[:, 2]
    same_session = recv_session[:, None] == recv_session[None, :]
    scores = jnp.einsum("qhd,khd->hqk", queries, keys_all, preferred_element_type=f32) * score_scale
    scores = jnp.where(same_session[None], scores, -1e30)
    row_max = jnp.max(scores, axis=2, keepdims=True)
    shifted = jnp.exp(scores - row_max)
    mixing = shifted / jnp.sum(shifted, axis=2, keepdims=True)
    mixing_b = mixing.astype(bf16)
    attended = jnp.einsum("hqk,khd->qhd", mixing_b, values, preferred_element_type=f32).astype(bf16)
    attended = attended.reshape(slot_count, model_width)
    hidden = as_float + jnp.dot(attended, w_out, preferred_element_type=f32)
    member = (recv_session[None, :] == lax.broadcasted_iota(jnp.int32, (SESS, 1), 0)).astype(f32)
    counts = jnp.maximum(jnp.sum(member, axis=1, keepdims=True), 1.0)
    pooled = jnp.dot(member, hidden, precision=lax.Precision.HIGHEST) / counts
    pooled_b = pooled.astype(bf16)
    logits = jnp.dot(pooled_b, w_head, preferred_element_type=f32)
    class_probs = jax.nn.softmax(logits, axis=1)
    target = (
        labels_here[:, None] == lax.broadcasted_iota(jnp.int32, (1, w_head.shape[1]), 1)
    ).astype(f32)
    dlogits = (class_probs - target) / SESS
    grad_head = jnp.dot(pooled_b.astype(f32).T, dlogits, precision=lax.Precision.HIGHEST)
    dpooled = jnp.dot(dlogits, w_head.astype(f32).T, precision=lax.Precision.HIGHEST)
    dhidden = jnp.dot(member.T, dpooled / counts, precision=lax.Precision.HIGHEST)
    dhidden_b = dhidden.astype(bf16)
    grad_out = jnp.einsum("rk,rd->kd", attended, dhidden_b, preferred_element_type=f32)
    dattended = jnp.einsum("rd,kd->rk", dhidden_b, w_out, preferred_element_type=f32).astype(bf16)
    dattended = dattended.reshape(slot_count, HEADS, head_dim)
    dmixing = jnp.einsum("qhd,khd->hqk", dattended, values, preferred_element_type=f32)
    dvalues = jnp.einsum("hqk,qhd->khd", mixing_b, dattended, preferred_element_type=f32)
    dscores = (
        mixing * (dmixing - jnp.sum(mixing * dmixing, axis=2, keepdims=True)) * score_scale
    ).astype(bf16)
    dqueries = jnp.einsum("hqk,khd->qhd", dscores, keys_all, preferred_element_type=f32)
    dkeys = jnp.einsum("hqk,qhd->khd", dscores, queries, preferred_element_type=f32)
    dprojected = (
        jnp.stack([dqueries, dkeys, dvalues], axis=1)
        .reshape(slot_count, 3 * model_width)
        .astype(bf16)
    )
    grad_project = jnp.einsum("rk,rd->kd", norm_in, dprojected, preferred_element_type=f32)
    dnorm = jnp.einsum("rd,kd->rk", dprojected, w_project, preferred_element_type=f32)
    grad_gain = jnp.sum(dnorm * as_float * inverse, axis=0)
    scaled = dnorm * gain_f
    d_input = (
        inverse * scaled
        - as_float
        * (inverse * inverse * inverse)
        * jnp.mean(as_float * scaled, axis=1, keepdims=True)
        + dhidden
    )
    return (logits, d_input.astype(bf16), (grad_gain, grad_project, grad_out, grad_head))


def body(
    packet_bytes,
    owner_index,
    session_id,
    class_label,
    byte_table,
    w_conv,
    norm_gain,
    w_project,
    w_out,
    w_head,
):
    f32 = jnp.float32
    bf16 = jnp.bfloat16
    groups = lax.axis_size("dp")
    packet_count = packet_bytes.shape[0]
    slot_count = 2 * packet_count
    capacity = slot_count // groups
    positions = BYTES // KERNEL
    window_width = w_conv.shape[0]
    model_width = w_conv.shape[1]
    windows = windows_of(packet_bytes, byte_table).reshape(-1, window_width)
    conv = jnp.dot(windows, w_conv, preferred_element_type=f32).reshape(
        packet_count, positions, model_width
    )
    embedding = jnp.mean(jax.nn.silu(conv), axis=1).astype(bf16)
    targets = lax.broadcasted_iota(jnp.int32, (1, groups), 1)
    chosen = (owner_index[:, None] == targets).astype(jnp.int32)
    send_rank = jnp.sum((jnp.cumsum(chosen, axis=0) - 1) * chosen, axis=1)
    send_slot = owner_index * capacity + send_rank
    outgoing = jnp.zeros((slot_count, model_width), bf16).at[send_slot].set(embedding)
    out_session = jnp.full((slot_count,), -1.0, bf16).at[send_slot].set(session_id.astype(bf16))
    incoming, in_session = (
        lax.all_to_all(
            outgoing.reshape(groups, capacity, model_width),
            "dp",
            split_axis=0,
            concat_axis=0,
            tiled=True,
        ),
        lax.all_to_all(
            out_session.reshape(groups, capacity), "dp", split_axis=0, concat_axis=0, tiled=True
        ),
    )
    received = incoming.reshape(slot_count, model_width)
    recv_session = in_session.reshape(slot_count).astype(jnp.int32)
    logits, d_input, owner_grads = session_layer(
        received, recv_session, class_label, norm_gain, w_project, w_out, w_head
    )
    returned = lax.all_to_all(
        d_input.reshape(groups, capacity, model_width),
        "dp",
        split_axis=0,
        concat_axis=0,
        tiled=True,
    )
    dembedding = returned.reshape(slot_count, model_width)[send_slot]
    dconv = (
        (dembedding.astype(f32)[:, None, :] / positions * silu_slope(conv))
        .astype(bf16)
        .reshape(-1, model_width)
    )
    grad_conv = jnp.einsum("rk,rd->kd", windows, dconv, preferred_element_type=f32)
    dwindows = jnp.einsum("rd,kd->rk", dconv, w_conv, preferred_element_type=f32).astype(bf16)
    chan_count = byte_table.shape[1]
    dwindows = dwindows.reshape(packet_count // 16, 16 * BYTES, chan_count)
    code_blocks = packet_bytes.reshape(packet_count // 16, 16 * BYTES)

    def add_block(total, item):
        block_codes, block_grad = item
        onehot = (block_codes[:, None] == lax.broadcasted_iota(jnp.int32, (1, 256), 1)).astype(bf16)
        return (
            total + jnp.einsum("rv,rc->vc", onehot, block_grad, preferred_element_type=f32),
            None,
        )

    grad_table, unused = lax.scan(
        add_block, jnp.zeros((256, chan_count), f32), (code_blocks, dwindows)
    )
    grads = (grad_table, grad_conv, owner_grads[0], owner_grads[1], owner_grads[2], owner_grads[3])
    totals = lax.psum((grads[0], grads[1], grads[2], grads[3], grads[4], grads[5]), ("dp", "rep"))
    return (logits, totals[0], totals[1], totals[2], totals[3], totals[4], totals[5])


def solution(mesh):
    in_specs = (
        P(("dp", "rep"), None),
        P(("dp", "rep")),
        P(("dp", "rep")),
        P(("dp", "rep")),
        P(),
        P(),
        P(),
        P(),
        P(),
        P(),
    )
    out_specs = (P(("dp", "rep"), None), P(), P(), P(), P(), P(), P())
    return jax.shard_map(body, mesh=mesh, in_specs=in_specs, out_specs=out_specs, check_vma=False)
```

profile of v0, /device:TPU:0, one launch (start us, length us, event | category | flops | bytes accessed | tf_op | source)
XLA Modules:
  0.0 378.5 jit_solution(12326877280065003547)
XLA Ops:
  10.4 1.3 scatter_custom_fusion
  12.4 7.3 %all-to-all-start = ((bf16[8,1,32]{2,1,0:T(2,128)(2,1)}), bf16[8,1,32]{2,1,0:T(2,128)(2,1)S(1)}, u32[]{:S(2)}, u32[]{:S(2)}) async-start(bf16[8,1,32]{2,1,0:T(2,128)(2,1)} %all_to_all.16), calls=%async_computation | async-start | bytes 8192 | tf_op jit(solution)/shard_map/all_to_all | solution.py:141
  19.7 26.4 %while.21 = (s32[]{:T(128)}, bf16[8,16,256,64]{2,3,1,0:T(8,128)(2,1)}, s32[8,16,256]{2,1,0:T(8,128)}, bf16[256,64]{0,1:T(8,128)(2,1)}, s32[]{:T(128)}) while((s32[]{:T(128)}, bf16[8,16,256,64]{2,3,1,0:T(8,128)(2,1)}, s32[8,16,256]{2,1,0:T(8,128)}, bf16[256,64]{0,1:T(8,128)(2,1)}, s32[]{:T(128)}) %tuple.55), condition=%wide.region_4.5_spmd, body=%wide.region_3.4_spmd.sunk | while | flops 135528448 | bytes 606285 | solution.py:29
  20.4 2.6 fusion.106
  23.7 2.6 fusion.106
  27.0 2.6 fusion.106
  30.3 2.6 fusion.106
  33.6 2.6 fusion.106
  36.9 2.6 fusion.106
  40.2 2.6 fusion.106
  43.5 2.6 fusion.106
  46.1 8.5 %copy.48 = bf16[8,16,256,64]{3,2,1,0:T(8,128)(2,1)} copy(bf16[8,16,256,64]{2,3,1,0:T(8,128)(2,1)} %get-tuple-element.51) | data formatting | bytes 8388608 | tf_op jit(solution)/shard_map/while | solution.py:29
  54.6 11.8 %dot_general.68 = bf16[128,32,512]{2,1,0:T(8,128)(2,1)} reshape(bf16[8,16,256,64]{3,2,1,0:T(8,128)(2,1)} %copy.48) | data formatting | bytes 8388608 | tf_op jit(solution)/shard_map/dot_general | solution.py:123
  66.4 14.6 %multiply_reduce_fusion = (f32[128,512]{1,0:T(8,128)S(1)}, f32[128,32,512]{2,0,1:T(8,128)}) fusion(bf16[512,512]{1,0:T(8,128)(2,1)S(1)} %copy-done.29, bf16[128,32,512]{2,1,0:T(8,128)(2,1)} %dot_general.68), kind=kOutput, calls=%fused_computation.22 | convolution fusion | flops 2157903872 | bytes 13369344 | tf_op jit(solution)/shard_map/dot_general | solution.py:123
  81.6 11.8 %reshape_reshape.3 = bf16[4096,512]{1,0:T(8,128)(2,1)} reshape(bf16[8,16,256,64]{3,2,1,0:T(8,128)(2,1)} %copy.48) | data formatting | bytes 8388608 | tf_op jit(solution)/shard_map/reshape;reshape | solution.py:122
  93.4 1.7 scatter_custom_fusion.1
  95.1 6.0 %all-to-all-start.1 = ((bf16[8,32,512]{2,1,0:T(8,128)(2,1)}), bf16[8,32,512]{2,1,0:T(8,128)(2,1)S(1)}, u32[]{:S(2)}, u32[]{:S(2)}) async-start(bf16[8,32,512]{2,1,0:T(8,128)(2,1)} %bitcast.5), calls=%async_computation.1 | async-start | bytes 524288 | tf_op jit(solution)/shard_map/all_to_all | solution.py:134
  102.6 7.0 %all-to-all-done.1 = bf16[8,32,512]{2,1,0:T(8,128)(2,1)S(1)} async-done(((bf16[8,32,512]{2,1,0:T(8,128)(2,1)}), bf16[8,32,512]{2,1,0:T(8,128)(2,1)S(1)}, u32[]{:S(2)}, u32[]{:S(2)}) %all-to-all-start.1) | async-done | bytes 262176 | tf_op jit(solution)/shard_map/all_to_all | solution.py:134
  112.0 3.0 fusion.75
  115.0 2.0 convolution_convert_fusion.3
  120.0 1.3 fusion.56
  122.1 2.8 convolution_bitcast_fusion
  124.9 1.9 fusion.53
  126.8 5.0 %fusion.26 = bf16[256,1,8,64]{0,3,2,1:T(8,128)(2,1)} fusion(f32[8,256,256]{1,2,0:T(8,128)} %fusion.53, bf16[256,3,8,64]{0,3,2,1:T(8,128)(2,1)S(1)} %bitcast.141, f32[8,256,256]{1,2,0:T(8,128)} %get-tuple-element.94, f32[8,256]{1,0:T(8,128)} %copy-done.31), kind=kOutput, calls=%fused_computation.37 | convolution fusion | flops 70781184 | bytes 8929280 | tf_op jit(solution)/shard_map/hqk,khd->qhd/dot_general | solution.py:80
  131.8 5.0 %fusion.29 = bf16[256,1,8,64]{0,3,2,1:T(8,128)(2,1)} fusion(f32[8,256,256]{1,2,0:T(8,128)} %fusion.53, bf16[256,3,8,64]{0,3,2,1:T(8,128)(2,1)S(1)} %bitcast.142, f32[8,256,256]{1,2,0:T(8,128)} %get-tuple-element.94, f32[8,256]{1,0:T(8,128)S(1)} %copy-done.32), kind=kOutput, calls=%fused_computation.38 | convolution fusion | flops 70781184 | bytes 8929280 | tf_op jit(solution)/shard_map/hqk,qhd->khd/dot_general | solution.py:81
  138.0 1.5 fusion.49
  140.5 3.4 all-to-all-start.2
  145.4 2.3 fusion.78
  147.7 4.7 %all-to-all-done.2 = bf16[8,32,512]{2,1,0:T(8,128)(2,1)S(1)} async-done(((bf16[8,32,512]{2,1,0:T(8,128)(2,1)}), bf16[8,32,512]{2,1,0:T(8,128)(2,1)S(1)}, u32[]{:S(2)}, u32[]{:S(2)}) %all-to-all-start.2) | async-done | bytes 262176 | tf_op jit(solution)/shard_map/all_to_all | solution.py:150
  153.5 5.0 %multiply_convert_fusion = bf16[128,32,512]{2,0,1:T(8,128)(2,1)S(1)} fusion(f32[128,32,512]{2,0,1:T(8,128)} %get-tuple-element.92, f32[128,512]{1,0:T(8,128)S(1)} %convert_multiply_fusion.2), kind=kLoop, calls=%fused_computation.21 | loop fusion | flops 18874368 | bytes 12845056 | tf_op jit(solution)/shard_map/convert_element_type | solution.py:160
  158.5 2.4 copy.56
  160.9 4.4 %convolution_convert_fusion = bf16[4096,512]{1,0:T(8,128)(2,1)} fusion(bf16[4096,512]{1,0:T(8,128)(2,1)S(1)} %bitcast.132, bf16[512,512]{1,0:T(8,128)(2,1)S(1)} %copy-done.30), kind=kOutput, calls=%fused_computation.24 | convolution fusion | flops 2149580800 | bytes 8912896 | tf_op jit(solution)/shard_map/rd,kd->rk/dot_general | solution.py:164
  165.2 3.3 fusion.77
  168.6 11.2 %reshape.174 = bf16[8,4096,64]{2,1,0:T(8,128)(2,1)} reshape(bf16[4096,512]{1,0:T(8,128)(2,1)} %convolution_convert_fusion) | data formatting | bytes 8388608 | tf_op jit(solution)/shard_map/reshape | solution.py:166
  179.8 29.5 %while.22 = (s32[]{:T(128)}, f32[256,64]{0,1:T(8,128)S(1)}, s32[8,4096]{1,0:T(8,128)S(1)}, bf16[8,4096,64]{2,1,0:T(8,128)(2,1)}, s32[]{:T(128)}, /*index=5*/s32[]{:T(128)}) while((s32[]{:T(128)}, f32[256,64]{0,1:T(8,128)S(1)}, s32[8,4096]{1,0:T(8,128)S(1)}, bf16[8,4096,64]{2,1,0:T(8,128)(2,1)}, s32[]{:T(128)}, ...), condition=%wide.region_16.17_spmd.clone, body=%wide.region_15.16_spmd.clone.sunk | while | flops 135299072 | bytes 1228895 | solution.py:177
  179.8 3.6 fusion.108
  183.5 3.6 fusion.108
  187.2 3.6 fusion.108
  190.9 3.6 fusion.108
  194.6 3.6 fusion.108
  198.2 3.6 fusion.108
  201.9 3.6 fusion.108
  205.6 3.6 fusion.108
  209.9 39.5 %psum.44 = f32[512]{0:T(512)} all-reduce(f32[512]{0:T(512)S(1)} %get-tuple-element.68), channel_id=1, replica_groups=mesh['dp'=8,'rep'=4] {'dp','rep'}, use_global_device_ids=true, to_apply=%region_20.21 | all-reduce | flops 512 | bytes 4096 | tf_op jit(solution)/shard_map/psum | solution.py:181
  249.5 112.7 %all-reduce.3.cloned.1.call-done = (f32[256,64]{0,1:T(8,128)}, f32[512,512]{1,0:T(8,128)}, f32[512,1536]{1,0:T(8,128)}, f32[512,512]{1,0:T(8,128)}, f32[512,128]{1,0:T(8,128)}) async-done(((f32[256,64]{0,1:T(8,128)}, f32[512,512]{1,0:T(8,128)}, f32[512,1536]{1,0:T(8,128)}, f32[512,512]{1,0:T(8,128)}, f32[512,128]{1,0:T(8,128)}), (f32[256,64]{0,1:T(8,128)}, f32[512,512]{1,0:T(8,128)}, f32[512,1536]{1,0:T(8,128)}, ...) | async-done | bytes 5570576 | tf_op jit(solution)/shard_map/psum | solution.py:181
  362.2 1.5 copy.84
  363.7 2.3 copy.85
  365.9 3.9 %copy.86 = f32[512,1536]{1,0:T(8,128)} copy(f32[512,1536]{1,0:T(8,128)} %get-tuple-element.187) | data formatting | bytes 6291456
  (124 shorter events, 25.0 us)
Async XLA Ops:
  7.2 103.9 %copy-start = (bf16[512,1536]{1,0:T(8,128)(2,1)S(1)}, bf16[512,1536]{1,0:T(8,128)(2,1)}, u32[]{:S(2)}) copy-start(bf16[512,1536]{1,0:T(8,128)(2,1)} %param.21) | copy-start | bytes 4718596
  12.4 82.7 %all-to-all-start = ((bf16[8,1,32]{2,1,0:T(2,128)(2,1)}), bf16[8,1,32]{2,1,0:T(2,128)(2,1)S(1)}, u32[]{:S(2)}, u32[]{:S(2)}) async-start(bf16[8,1,32]{2,1,0:T(2,128)(2,1)} %all_to_all.16), calls=%async_computation | async-start | bytes 8192 | tf_op jit(solution)/shard_map/all_to_all | solution.py:141
  54.6 11.8 %copy-start.29 = (bf16[512,512]{1,0:T(8,128)(2,1)S(1)}, bf16[512,512]{1,0:T(8,128)(2,1)}, u32[]{:S(2)}) copy-start(bf16[512,512]{1,0:T(8,128)(2,1)} %param.19) | copy-start | bytes 1572868
  66.4 15.2 %copy-start.6 = (s32[8,16,256]{2,1,0:T(8,128)S(1)}, s32[8,16,256]{2,1,0:T(8,128)}, u32[]{:S(2)}) copy-start(s32[8,16,256]{2,1,0:T(8,128)} %get-tuple-element.211) | copy-start | bytes 393220
  81.6 11.8 %copy-start.25 = (bf16[512]{0:T(512)(128)(2,1)S(1)}, bf16[512]{0:T(512)(128)(2,1)}, u32[]{:S(2)}) copy-start(bf16[512]{0:T(512)(128)(2,1)} %param.20) | copy-start | bytes 3076
  93.4 16.5 %copy-start.15 = (f32[512]{0:T(512)}, f32[512]{0:T(512)S(1)}, u32[]{:S(2)}) copy-start(f32[512]{0:T(512)S(1)} %convert_element_type.118) | copy-start | bytes 6148
  95.1 14.5 %all-to-all-start.1 = ((bf16[8,32,512]{2,1,0:T(8,128)(2,1)}), bf16[8,32,512]{2,1,0:T(8,128)(2,1)S(1)}, u32[]{:S(2)}, u32[]{:S(2)}) async-start(bf16[8,32,512]{2,1,0:T(8,128)(2,1)} %bitcast.5), calls=%async_computation.1 | async-start | bytes 524288 | tf_op jit(solution)/shard_map/all_to_all | solution.py:134
  101.2 8.4 %copy-start.17 = (s32[256]{0:T(256)}, s32[256]{0:T(256)S(1)}, u32[]{:S(2)}) copy-start(s32[256]{0:T(256)S(1)} %reshape.175) | copy-start | bytes 3076
  109.8 0.6 copy-start.13
  110.4 0.6 copy-start.19
  115.0 2.0 copy-start.31
  115.0 2.0 copy-start.3
  115.0 2.3 copy-start.18
  115.0 2.4 copy-start.28
  117.0 0.9 copy-start.8
  117.0 1.7 copy-start.26
  118.1 0.6 copy-start.9
  118.1 0.9 copy-start.21
  118.7 0.5 copy-start.23
  122.1 2.8 copy-start.4
  126.8 5.0 %copy-start.32 = (f32[8,256]{1,0:T(8,128)S(1)}, f32[8,256]{1,0:T(8,128)}, u32[]{:S(2)}) copy-start(f32[8,256]{1,0:T(8,128)} %copy-done.31) | copy-start | bytes 24580
  138.0 1.6 copy-start.20
  138.0 1.6 copy-start.16
  138.0 6.2 %copy-start.14 = (f32[8,32]{1,0:T(8,128)S(1)}, f32[8,32]{1,0:T(8,128)}, u32[]{:S(2)}) copy-start(f32[8,32]{1,0:T(8,128)} %copy-done.13) | copy-start | bytes 3076
  139.5 4.8 %copy-start.10 = (f32[16,128]{1,0:T(8,128)S(1)}, f32[16,128]{1,0:T(8,128)}, u32[]{:S(2)}) copy-start(f32[16,128]{1,0:T(8,128)} %copy-done.9) | copy-start | bytes 24580
  139.5 4.8 %copy-start.22 = (f32[16]{0:T(128)S(1)}, f32[16]{0:T(128)}, u32[]{:S(2)}) copy-start(f32[16]{0:T(128)} %copy-done.21) | copy-start | bytes 196
  139.6 4.8 %copy-start.24 = (f32[16]{0:T(128)S(1)}, f32[16]{0:T(128)}, u32[]{:S(2)}) copy-start(f32[16]{0:T(128)} %copy-done.23) | copy-start | bytes 196
  139.6 4.8 %copy-start.27 = (s32[16]{0:T(128)S(1)}, s32[16]{0:T(128)}, u32[]{:S(2)}) copy-start(s32[16]{0:T(128)} %param.17) | copy-start | bytes 196
  140.5 12.0 %all-to-all-start.2 = ((bf16[8,32,512]{2,1,0:T(8,128)(2,1)}), bf16[8,32,512]{2,1,0:T(8,128)(2,1)S(1)}, u32[]{:S(2)}, u32[]{:S(2)}) async-start(bf16[8,32,512]{2,1,0:T(8,128)(2,1)} %bitcast.21), calls=%async_computation.2 | async-start | bytes 524288 | tf_op jit(solution)/shard_map/all_to_all | solution.py:150
  143.9 218.2 %all-reduce.3.cloned.1.call-start = ((), (), s32[]{:S(2)}) async-start(), calls=%async_computation.3 | async-start | bytes 11141120 | tf_op jit(solution)/shard_map/psum | solution.py:181
  158.5 2.4 copy-start.30
  160.9 4.4 %copy-start.2 = (bf16[4096,512]{1,0:T(8,128)(2,1)S(1)}, bf16[4096,512]{1,0:T(8,128)(2,1)}, u32[]{:S(2)}) copy-start(bf16[4096,512]{1,0:T(8,128)(2,1)} %reshape_reshape.3) | copy-start | bytes 12582916
  168.6 11.2 %copy-start.11 = (f32[256,64]{0,1:T(8,128)S(1)}, f32[256,64]{0,1:T(8,128)}, u32[]{:S(2)}) copy-start(f32[256,64]{0,1:T(8,128)} %custom-call) | copy-start | bytes 196612
  209.3 0.6 copy-start.12
  365.9 3.9 %copy-start.5 = (f32[512,512]{1,0:T(8,128)S(1)}, f32[512,512]{1,0:T(8,128)}, u32[]{:S(2)}) copy-start(f32[512,512]{1,0:T(8,128)} %get-tuple-element.188) | copy-start | bytes 3145732
  365.9 5.7 %copy-start.1 = (bf16[512,1536]{1,0:T(8,128)(2,1)S(1)}, bf16[512,1536]{1,0:T(8,128)(2,1)}, u32[]{:S(2)}) copy-start(bf16[512,1536]{1,0:T(8,128)(2,1)} %param.21) | copy-start | bytes 4718596
  369.8 1.1 copy-start.7
Sparse Core Ops, SparseCore 0:
  210.1 152.0 all-reduce.2
where the time goes:
time: 382 us; the launch traced here: 378 us
  waiting for transfers between devices  125 us (33%)
  matrix products  100 us (26%)
  local copies, waits for them, and re-layouts  68 us (18%)
  blocking collectives  39.5 us (10%)
  starting transfers between devices  17 us (4%)
  other arithmetic  14.6 us (4%)
  between operations  14.5 us (4%)
    psum x1, waiting for transfers between devices, body(): lax.psum((grads[0], grads[1], grads[2], grads[3], grads[4], grads[5]), ('...  113 us
    psum x1, blocking collectives, body(): lax.psum((grads[0], grads[1], grads[2], grads[3], grads[4], grads[5]), ('...  39.5 us
    dot_general x8, matrix products, add_block(): jnp.einsum('rv,rc->vc', onehot, block_grad, preferred_element_type=f32)  29.1 us
    dot_general x8, matrix products, lookup_block(): jnp.einsum('pbv,vc->pbc', onehot, byte_table, preferred_element_type=jnp....  20.6 us
    dot_general x1, matrix products, body(): jnp.dot(windows, w_conv, preferred_element_type=f32)  14.6 us
    unnamed x71, local copies, waits for them, and re-layouts  12.2 us
    dot_general x1, local copies, waits for them, and re-layouts, body(): jnp.dot(windows, w_conv, preferred_element_type=f32)  11.8 us
    another operation x1, local copies, waits for them, and re-layouts, body(): windows = windows_of(packet_bytes, byte_table).reshape(-1, window_width)  11.8 us
  transfers between devices with their start and end apart: 4, of which 3 were waited for; matrix products, arithmetic and copies ran while one was open for 21% of the time, Pallas kernels for 0%

commit v1 on v0

--- a/solution.py
+++ b/solution.py
@@ -178,7 +178,9 @@
         add_block, jnp.zeros((256, chan_count), f32), (code_blocks, dwindows)
     )
     grads = (grad_table, grad_conv, owner_grads[0], owner_grads[1], owner_grads[2], owner_grads[3])
-    totals = lax.psum((grads[0], grads[1], grads[2], grads[3], grads[4], grads[5]), ("dp", "rep"))
+    totals = lax.psum(
+        lax.psum((grads[0], grads[1], grads[2], grads[3], grads[4], grads[5]), "rep"), "dp"
+    )
     return (logits, totals[0], totals[1], totals[2], totals[3], totals[4], totals[5])
 
 

time: 382 us -> 536 us (1.40)
  waiting for transfers between devices: 125 us -> 290 us
  blocking collectives: 39.5 us -> 28.7 us
    psum x1 -> x2, waiting for transfers between devices: 113 us -> 279 us  [the longest x1 171 us: body(): lax.psum(lax.psum((grads[0], grads[1], grads[2], grads[3], grads[4], grad...]
    psum x1 -> x2, blocking collectives: 39.5 us -> 28.7 us  [the longest x1 22.8 us: body(): lax.psum(lax.psum((grads[0], grads[1], grads[2], grads[3], grads[4], grad...]
    unnamed x71 -> x73, local copies, waits for them, and re-layouts: 12.2 us -> 11.2 us
  transfers between devices with their start and end apart: 4 -> 5, of which waited for: 3 -> 4; matrix products, arithmetic and copies ran while one was open for 21% -> 15% of each run, Pallas kernels for 0% -> 0%
where the time goes in v1:
time: 536 us; the launch traced here: 533 us
  waiting for transfers between devices  290 us (54%)
  matrix products  100 us (19%)
  local copies, waits for them, and re-layouts  67 us (12%)
  blocking collectives  28.7 us (5%)
  starting transfers between devices  17 us (3%)
  other arithmetic  15.1 us (3%)
  between operations  14.5 us (3%)
    psum x1, waiting for transfers between devices, body(): lax.psum(lax.psum((grads[0], grads[1], grads[2], grads[3], grads[4], grad...  171 us
    psum x1, waiting for transfers between devices, body(): lax.psum((grads[0], grads[1], grads[2], grads[3], grads[4], grads[5]), 'r...  108 us
    dot_general x8, matrix products, add_block(): jnp.einsum('rv,rc->vc', onehot, block_grad, preferred_element_type=f32)  29.1 us
    psum x1, blocking collectives, body(): lax.psum(lax.psum((grads[0], grads[1], grads[2], grads[3], grads[4], grad...  22.8 us
    dot_general x8, matrix products, lookup_block(): jnp.einsum('pbv,vc->pbc', onehot, byte_table, preferred_element_type=jnp....  20.6 us
    dot_general x1, matrix products, body(): jnp.dot(windows, w_conv, preferred_element_type=f32)  14.6 us
    dot_general x1, local copies, waits for them, and re-layouts, body(): jnp.dot(windows, w_conv, preferred_element_type=f32)  11.8 us
    another operation x1, local copies, waits for them, and re-layouts, body(): windows = windows_of(packet_bytes, byte_table).reshape(-1, window_width)  11.8 us
  transfers between devices with their start and end apart: 5, of which 4 were waited for; matrix products, arithmetic and copies ran while one was open for 15% of the time, Pallas kernels for 0%

profile of v1, /device:TPU:0, one launch (start us, length us, event | category | flops | bytes accessed | tf_op | source)
XLA Modules:
  0.0 533.1 jit_solution(7274601019604218645)
XLA Ops:
  12.4 7.3 %all-to-all-start = ((bf16[8,1,32]{2,1,0:T(2,128)(2,1)}), bf16[8,1,32]{2,1,0:T(2,128)(2,1)S(1)}, u32[]{:S(2)}, u32[]{:S(2)}) async-start(bf16[8,1,32]{2,1,0:T(2,128)(2,1)} %all_to_all.16), calls=%async_computation | async-start | bytes 8192 | tf_op jit(solution)/shard_map/all_to_all | solution.py:141
  19.7 26.4 %while.21 = (s32[]{:T(128)}, bf16[8,16,256,64]{2,3,1,0:T(8,128)(2,1)}, s32[8,16,256]{2,1,0:T(8,128)}, bf16[256,64]{0,1:T(8,128)(2,1)}, s32[]{:T(128)}) while((s32[]{:T(128)}, bf16[8,16,256,64]{2,3,1,0:T(8,128)(2,1)}, s32[8,16,256]{2,1,0:T(8,128)}, bf16[256,64]{0,1:T(8,128)(2,1)}, s32[]{:T(128)}) %tuple.57), condition=%wide.region_4.5_spmd, body=%wide.region_3.4_spmd.sunk | while | flops 135528448 | bytes 606285 | solution.py:29
  20.4 2.6 fusion.106
  23.7 2.6 fusion.106
  27.0 2.6 fusion.106
  30.3 2.6 fusion.106
  33.6 2.6 fusion.106
  36.9 2.6 fusion.106
  40.2 2.6 fusion.106
  43.5 2.6 fusion.106
  46.1 8.5 %copy.48 = bf16[8,16,256,64]{3,2,1,0:T(8,128)(2,1)} copy(bf16[8,16,256,64]{2,3,1,0:T(8,128)(2,1)} %get-tuple-element.51) | data formatting | bytes 8388608 | tf_op jit(solution)/shard_map/while | solution.py:29
  54.6 11.8 %dot_general.68 = bf16[128,32,512]{2,1,0:T(8,128)(2,1)} reshape(bf16[8,16,256,64]{3,2,1,0:T(8,128)(2,1)} %copy.48) | data formatting | bytes 8388608 | tf_op jit(solution)/shard_map/dot_general | solution.py:123
  66.4 14.6 %multiply_reduce_fusion = (f32[128,512]{1,0:T(8,128)S(1)}, f32[128,32,512]{2,0,1:T(8,128)}) fusion(bf16[512,512]{1,0:T(8,128)(2,1)S(1)} %copy-done.30, bf16[128,32,512]{2,1,0:T(8,128)(2,1)} %dot_general.68), kind=kOutput, calls=%fused_computation.22 | convolution fusion | flops 2157903872 | bytes 13369344 | tf_op jit(solution)/shard_map/dot_general | solution.py:123
  81.6 11.8 %reshape_reshape.3 = bf16[4096,512]{1,0:T(8,128)(2,1)} reshape(bf16[8,16,256,64]{3,2,1,0:T(8,128)(2,1)} %copy.48) | data formatting | bytes 8388608 | tf_op jit(solution)/shard_map/reshape;reshape | solution.py:122
  93.4 1.7 scatter_custom_fusion.1
  95.1 6.0 %all-to-all-start.1 = ((bf16[8,32,512]{2,1,0:T(8,128)(2,1)}), bf16[8,32,512]{2,1,0:T(8,128)(2,1)S(1)}, u32[]{:S(2)}, u32[]{:S(2)}) async-start(bf16[8,32,512]{2,1,0:T(8,128)(2,1)} %bitcast.5), calls=%async_computation.1 | async-start | bytes 524288 | tf_op jit(solution)/shard_map/all_to_all | solution.py:134
  102.6 7.0 %all-to-all-done.1 = bf16[8,32,512]{2,1,0:T(8,128)(2,1)S(1)} async-done(((bf16[8,32,512]{2,1,0:T(8,128)(2,1)}), bf16[8,32,512]{2,1,0:T(8,128)(2,1)S(1)}, u32[]{:S(2)}, u32[]{:S(2)}) %all-to-all-start.1) | async-done | bytes 262176 | tf_op jit(solution)/shard_map/all_to_all | solution.py:134
  111.5 3.0 fusion.75
  114.5 2.0 convolution_convert_fusion.3
  121.6 2.8 convolution_bitcast_fusion
  124.4 1.9 fusion.53
  126.3 5.0 fusion.26
  131.3 5.0 fusion.29
  137.5 1.5 fusion.49
  140.0 3.4 all-to-all-start.2
  144.9 2.3 fusion.78
  147.2 4.7 all-to-all-done.2
  152.9 5.0 multiply_convert_fusion
  157.9 2.4 copy.56
  160.3 4.4 convolution_convert_fusion
  164.7 3.3 fusion.77
  168.0 11.2 %reshape.174 = bf16[8,4096,64]{2,1,0:T(8,128)(2,1)} reshape(bf16[4096,512]{1,0:T(8,128)(2,1)} %convolution_convert_fusion) | data formatting | bytes 8388608 | tf_op jit(solution)/shard_map/reshape | solution.py:166
  179.2 29.5 %while.22 = (s32[]{:T(128)}, f32[256,64]{0,1:T(8,128)S(1)}, s32[8,4096]{1,0:T(8,128)S(1)}, bf16[8,4096,64]{2,1,0:T(8,128)(2,1)}, s32[]{:T(128)}, /*index=5*/s32[]{:T(128)}) while((s32[]{:T(128)}, f32[256,64]{0,1:T(8,128)S(1)}, s32[8,4096]{1,0:T(8,128)S(1)}, bf16[8,4096,64]{2,1,0:T(8,128)(2,1)}, s32[]{:T(128)}, ...), condition=%wide.region_16.17_spmd.clone, body=%wide.region_15.16_spmd.clone.sunk | while | flops 135299072 | bytes 1228895 | solution.py:177
  179.3 3.6 fusion.108
  183.0 3.6 fusion.108
  186.6 3.6 fusion.108
  190.3 3.6 fusion.108
  194.0 3.6 fusion.108
  197.7 3.6 fusion.108
  201.4 3.6 fusion.108
  205.1 3.6 fusion.108
  209.4 107.6 %all-reduce.7.cloned.1.call-done = (f32[256,64]{0,1:T(8,128)}, f32[512,512]{1,0:T(8,128)}, f32[512,1536]{1,0:T(8,128)}, f32[512,512]{1,0:T(8,128)}, f32[512,128]{1,0:T(8,128)}) async-done(((f32[256,64]{0,1:T(8,128)}, f32[512,512]{1,0:T(8,128)}, f32[512,1536]{1,0:T(8,128)}, f32[512,512]{1,0:T(8,128)}, f32[512,128]{1,0:T(8,128)}), (f32[256,64]{0,1:T(8,128)}, f32[512,512]{1,0:T(8,128)}, f32[512,1536]{1,0:T(8,128)}, ...) | async-done | bytes 5570576 | tf_op jit(solution)/shard_map/psum | solution.py:182
  317.1 5.9 %psum.88 = f32[512]{0:T(512)S(1)} all-reduce(f32[512]{0:T(512)S(1)} %get-tuple-element.68), channel_id=1, replica_groups=mesh['dp'=8,'rep'=4] {'rep'}, use_global_device_ids=true, to_apply=%region_22.23 | all-reduce | flops 512 | bytes 4096 | tf_op jit(solution)/shard_map/psum | solution.py:182
  323.0 22.8 %psum.89 = f32[512]{0:T(512)} all-reduce(f32[512]{0:T(512)S(1)} %psum.88), channel_id=1, replica_groups=mesh['dp'=8,'rep'=4] {'dp'}, use_global_device_ids=true, to_apply=%region_23.24 | all-reduce | flops 512 | bytes 4096 | tf_op jit(solution)/shard_map/psum | solution.py:181
  345.8 171.0 %all-reduce.5.cloned.1.call-done = (f32[256,64]{0,1:T(8,128)}, f32[512,512]{1,0:T(8,128)}, f32[512,1536]{1,0:T(8,128)}, f32[512,512]{1,0:T(8,128)}, f32[512,128]{1,0:T(8,128)}) async-done(((f32[256,64]{0,1:T(8,128)}, f32[512,512]{1,0:T(8,128)}, f32[512,1536]{1,0:T(8,128)}, f32[512,512]{1,0:T(8,128)}, f32[512,128]{1,0:T(8,128)}), (f32[256,64]{0,1:T(8,128)}, f32[512,512]{1,0:T(8,128)}, f32[512,1536]{1,0:T(8,128)}, ...) | async-done | bytes 5570576 | tf_op jit(solution)/shard_map/psum | solution.py:181
  516.8 1.5 copy.89
  518.3 2.3 copy.90
  520.6 3.9 copy.91
  (131 shorter events, 27.2 us)
Async XLA Ops:
  7.2 103.4 %copy-start = (bf16[512,1536]{1,0:T(8,128)(2,1)S(1)}, bf16[512,1536]{1,0:T(8,128)(2,1)}, u32[]{:S(2)}) copy-start(bf16[512,1536]{1,0:T(8,128)(2,1)} %param.21) | copy-start | bytes 4718596
  12.4 82.7 %all-to-all-start = ((bf16[8,1,32]{2,1,0:T(2,128)(2,1)}), bf16[8,1,32]{2,1,0:T(2,128)(2,1)S(1)}, u32[]{:S(2)}, u32[]{:S(2)}) async-start(bf16[8,1,32]{2,1,0:T(2,128)(2,1)} %all_to_all.16), calls=%async_computation | async-start | bytes 8192 | tf_op jit(solution)/shard_map/all_to_all | solution.py:141
  54.6 11.8 %copy-start.30 = (bf16[512,512]{1,0:T(8,128)(2,1)S(1)}, bf16[512,512]{1,0:T(8,128)(2,1)}, u32[]{:S(2)}) copy-start(bf16[512,512]{1,0:T(8,128)(2,1)} %param.19) | copy-start | bytes 1572868
  66.4 15.2 %copy-start.6 = (s32[8,16,256]{2,1,0:T(8,128)S(1)}, s32[8,16,256]{2,1,0:T(8,128)}, u32[]{:S(2)}) copy-start(s32[8,16,256]{2,1,0:T(8,128)} %get-tuple-element.232) | copy-start | bytes 393220
  81.6 11.8 %copy-start.26 = (bf16[512]{0:T(512)(128)(2,1)S(1)}, bf16[512]{0:T(512)(128)(2,1)}, u32[]{:S(2)}) copy-start(bf16[512]{0:T(512)(128)(2,1)} %param.20) | copy-start | bytes 3076
  93.4 17.0 %copy-start.15 = (f32[512]{0:T(512)}, f32[512]{0:T(512)S(1)}, u32[]{:S(2)}) copy-start(f32[512]{0:T(512)S(1)} %convert_element_type.118) | copy-start | bytes 6148
  95.1 14.5 %all-to-all-start.1 = ((bf16[8,32,512]{2,1,0:T(8,128)(2,1)}), bf16[8,32,512]{2,1,0:T(8,128)(2,1)S(1)}, u32[]{:S(2)}, u32[]{:S(2)}) async-start(bf16[8,32,512]{2,1,0:T(8,128)(2,1)} %bitcast.5), calls=%async_computation.1 | async-start | bytes 524288 | tf_op jit(solution)/shard_map/all_to_all | solution.py:134
  101.2 8.4 %copy-start.17 = (s32[256]{0:T(256)}, s32[256]{0:T(256)S(1)}, u32[]{:S(2)}) copy-start(s32[256]{0:T(256)S(1)} %reshape.175) | copy-start | bytes 3076
  109.8 0.6 copy-start.13
  109.9 0.6 copy-start.19
  114.5 2.0 copy-start.32
  114.5 2.0 copy-start.3
  114.5 2.3 copy-start.18
  114.5 2.4 copy-start.29
  116.4 0.9 copy-start.8
  116.5 1.7 copy-start.27
  117.6 0.6 copy-start.9
  117.6 0.9 copy-start.21
  118.2 0.6 copy-start.24
  121.6 2.8 copy-start.4
  126.3 5.0 copy-start.33
  137.5 1.6 copy-start.16
  137.5 1.6 copy-start.20
  137.5 1.6 copy-start.23
  137.5 6.2 %copy-start.14 = (f32[8,32]{1,0:T(8,128)S(1)}, f32[8,32]{1,0:T(8,128)}, u32[]{:S(2)}) copy-start(f32[8,32]{1,0:T(8,128)} %copy-done.13) | copy-start | bytes 3076
  139.0 4.8 copy-start.10
  139.0 4.8 copy-start.22
  139.0 4.8 copy-start.25
  139.0 4.8 copy-start.28
  140.0 12.0 %all-to-all-start.2 = ((bf16[8,32,512]{2,1,0:T(8,128)(2,1)}), bf16[8,32,512]{2,1,0:T(8,128)(2,1)S(1)}, u32[]{:S(2)}, u32[]{:S(2)}) async-start(bf16[8,32,512]{2,1,0:T(8,128)(2,1)} %bitcast.21), calls=%async_computation.2 | async-start | bytes 524288 | tf_op jit(solution)/shard_map/all_to_all | solution.py:150
  143.4 173.6 %all-reduce.7.cloned.1.call-start = ((), (), s32[]{:S(2)}) async-start(), calls=%async_computation.4 | async-start | bytes 11141120 | tf_op jit(solution)/shard_map/psum | solution.py:182
  157.9 2.4 copy-start.31
  160.3 4.4 copy-start.2
  168.0 11.2 %copy-start.11 = (f32[256,64]{0,1:T(8,128)S(1)}, f32[256,64]{0,1:T(8,128)}, u32[]{:S(2)}) copy-start(f32[256,64]{0,1:T(8,128)} %custom-call) | copy-start | bytes 196612
  208.7 0.6 copy-start.12
  209.4 307.4 %all-reduce.5.cloned.1.call-start = ((), (), s32[]{:S(2)}) async-start(), calls=%async_computation.3 | async-start | bytes 11141120 | tf_op jit(solution)/shard_map/psum | solution.py:181
  520.5 3.9 copy-start.5
  520.5 5.7 %copy-start.1 = (bf16[512,1536]{1,0:T(8,128)(2,1)S(1)}, bf16[512,1536]{1,0:T(8,128)(2,1)}, u32[]{:S(2)}) copy-start(bf16[512,1536]{1,0:T(8,128)(2,1)} %param.21) | copy-start | bytes 4718596
  524.5 1.1 copy-start.7
Sparse Core Ops, SparseCore 0:
  209.5 107.4 all-reduce.6
  321.9 194.8 all-reduce.4
